TPU v7x, 32 devices: a whole 2x2x4 slice. The times are simulated.
32 devices in a mesh: wide: 8 (over z, y), narrow: 4 (over x, core).
Axes of the slice: x: 2, y: 2, z: 4, core: 2. Of those that a mesh axis runs over, the one named last changes fastest.
Arguments:
- entry_factor: bfloat16 [288, 4, 64, 1024], P('wide', 'narrow'), may hold values from -6 to 6
- entry_panel: int32 [288, 4], P('wide', 'narrow'), may hold values from 0 to 1
- entry_target: int32 [288, 4], P('wide', 'narrow'), may hold values from 0 to 7, as said below
- entry_count: int32 [4, 8], P('narrow', 'wide'), may hold values from 1 to 36, 96 in all within a row
- panel_shared: bfloat16 [16, 64, 1024], P('wide', None, 'narrow'), may hold values from -0.1875 to 0.1875
- coupling: float32 [16, 64, 64], P('wide'), may hold values from -0.75 to 0.75
- probes: bfloat16 [32, 64, 1024], P('narrow'), may hold values from -6 to 6
Outputs:
- left_factor: float32 [32, 64, 1024], P('narrow', None, 'wide')
- right_factor: float32 [32, 64, 1024], P('narrow', None, 'wide')
Inputs may be any that keep to these rules, and one draw needn't show every extreme that they name: `entry_panel`: the local panel of an entry of any slot, live or not. `entry_target`: the local target of an entry; every target has at least one live entry. `entry_count`: the live slots of one device; for every owner the counts over the 8 wide indices sum to 96, and some device holds exactly 36.
All inputs are finite; a program needn't handle non-finite values.
Results may differ from a plain program's by a relative error of at most 0.0036.
Values may be sent and summed in bfloat16 or wider, within the bound.
A program may use at most 64 MiB of HBM per device.

v0:
```python
import math
import jax
import jax.numpy as jnp
from jax import lax
from jax.sharding import PartitionSpec as P


def shards(entry_factor, entry_panel, entry_target, entry_count, panel_shared, coupling, probes):
    highest = lax.Precision.HIGHEST
    factors = entry_factor[:, 0]
    slot_count = factors.shape[0]
    rank_dim = factors.shape[1]
    full_width = factors.shape[2]
    panel_count = panel_shared.shape[0]
    target_count = probes.shape[0]
    live_mask = (jnp.arange(slot_count) < entry_count[0, 0]).astype(jnp.float32)
    pick_panel = (entry_panel == jnp.arange(panel_count)[None, :]).astype(jnp.float32) * live_mask[
        :, None
    ]
    pick_target = (entry_target == jnp.arange(target_count)[None, :]).astype(jnp.float32)
    pair_pick = (pick_panel[:, :, None] * pick_target[:, None, :]).reshape(
        slot_count, panel_count * target_count
    )
    gathered = lax.all_gather(panel_shared, "narrow", axis=2, tiled=True)
    projected = jnp.einsum("drb,tkb->dtrk", gathered, probes, preferred_element_type=jnp.float32)
    coefficients = jnp.einsum("dij,dtjk->dtik", coupling, projected, precision=highest).astype(
        jnp.bfloat16
    )
    coeff_table = coefficients.reshape(panel_count * target_count, rank_dim * rank_dim)
    chosen = jnp.dot(
        pair_pick.astype(jnp.bfloat16), coeff_table, preferred_element_type=jnp.float32
    )
    chosen = chosen.astype(jnp.bfloat16).reshape(slot_count, rank_dim, rank_dim)
    contributions = jnp.einsum("eji,ejb->eib", chosen, factors, preferred_element_type=jnp.float32)
    sketch = jnp.einsum("et,eib->tib", pick_target, contributions, precision=highest)
    wide_count = lax.axis_size("wide")
    share_cols = full_width // wide_count
    sketch_part = lax.psum_scatter(sketch, "wide", scatter_dimension=2, tiled=True)
    gram_part = jnp.einsum("tib,tjb->tij", sketch_part, sketch_part, precision=highest)
    gram_matrix = lax.psum(gram_part, "wide")
    lower_factor = jnp.linalg.cholesky(gram_matrix)
    own_basis = jax.scipy.linalg.solve_triangular(lower_factor, sketch_part, lower=True)
    basis_round = lax.all_gather(own_basis.astype(jnp.bfloat16), "wide", axis=2, tiled=True)
    selected = jnp.einsum(
        "et,tkb->ekb",
        pick_target.astype(jnp.bfloat16),
        basis_round,
        preferred_element_type=jnp.float32,
    )
    selected = selected.astype(jnp.bfloat16)
    back_terms = jnp.einsum("eib,ekb->eik", factors, selected, preferred_element_type=jnp.float32)
    summed = jnp.einsum("ep,eik->pik", pair_pick, back_terms, precision=highest)
    summed = summed.reshape(panel_count, target_count, rank_dim, rank_dim)
    middle_terms = jnp.einsum("dtik,dij->dtkj", summed, coupling, precision=highest)
    partial_rows = jnp.einsum(
        "dtkj,djb->tkb", middle_terms, gathered.astype(jnp.float32), precision=highest
    )
    coeff_part = lax.psum_scatter(partial_rows, "wide", scatter_dimension=2, tiled=True)
    root_width = math.sqrt(full_width)
    return (own_basis * root_width, coeff_part / root_width)


def solution(mesh):
    placed = (
        P("wide", "narrow", None, None),
        P("wide", "narrow"),
        P("wide", "narrow"),
        P("narrow", "wide"),
        P("wide", None, "narrow"),
        P("wide", None, None),
        P("narrow", None, None),
    )
    return jax.shard_map(
        shards,
        mesh=mesh,
        in_specs=placed,
        out_specs=(P("narrow", None, "wide"), P("narrow", None, "wide")),
        check_vma=False,
    )
```

profile of v0, /device:TPU:0, one launch (start us, length us, event | category | flops | bytes accessed | tf_op | source)
XLA Modules:
  0.0 399.1 jit_solution(11624132694384365650)
XLA Ops:
  7.2 0.7 fusion.36
  8.0 7.4 %all_gather.6 = bf16[2,64,1024]{2,1,0:T(8,128)(2,1)S(1)} all-gather(bf16[2,64,256]{2,1,0:T(8,128)(2,1)} %param.11), channel_id=1, replica_groups=mesh['wide'=8,'narrow'=4] {'narrow'}, dimensions={2}, use_global_device_ids=true | all-gather | bytes 327680 | tf_op jit(solution)/shard_map/all_gather | solution.py:24
  15.4 0.5 convolution_bitcast_fusion.1
  15.9 0.3 copy-done.1
  16.1 1.4 fusion.14
  17.6 0.2 copy.23
  17.7 0.3 reshape.98
  18.7 0.7 compare_select_fusion
  19.3 0.3 convolution_convert_fusion
  19.6 0.6 reshape.99
  20.3 3.8 fusion.4
  24.1 10.1 %fusion = f32[8,64,1024]{2,0,1:T(8,128)} fusion(f32[36,64,1024]{2,1,0:T(8,128)S(1)} %fusion.4, s32[36]{0:T(128)S(1)} %bitcast.78), kind=kOutput, calls=%fused_computation | convolution fusion | flops 226492704 | bytes 11534480 | tf_op jit(solution)/shard_map/et,eib->tib/dot_general | solution.py:35
  34.2 0.0 all-reduce.2.cloned.1.call-start
  34.3 70.3 %reduce-scatter.3.cloned.1.call-done = f32[8,64,128]{2,0,1:T(8,128)} async-done(((f32[8,64,1024]{2,0,1:T(8,128)}), f32[8,64,128]{2,0,1:T(8,128)}) %reduce-scatter.3.cloned.1.call-update) | async-done | bytes 262160 | tf_op jit(solution)/shard_map/reduce_scatter | solution.py:38
  104.5 2.3 fusion.25
  106.9 71.6 %all-reduce.2.cloned.1.call-done = f32[8,64,64]{1,2,0:T(8,128)} async-done(((f32[8,64,64]{1,2,0:T(8,128)}), f32[8,64,64]{1,2,0:T(8,128)}) %all-reduce.2.cloned.1.call-update) | async-done | bytes 131088 | tf_op jit(solution)/shard_map/psum | solution.py:40
  178.5 1.1 copy.29
  179.6 1.0 fusion.22
  180.6 46.9 %custom-call.8 = f32[8,64,64]{2,1,0:T(8,128)S(1)} custom-call(f32[8,64,64]{2,1,0:T(8,128)S(1)} %fusion.22), custom_call_target="Cholesky" | custom-call | tf_op jit(solution)/shard_map/jit(cholesky)/cholesky | solution.py:41
  227.5 0.1 compare_reduce_fusion
  227.6 0.1 select_bitcast_fusion
  227.8 39.3 %custom-call.9 = f32[8,1,64,64]{2,3,1,0:T(8,128)S(1)} custom-call(f32[8,1,64,64]{3,2,1,0:T(8,128)S(1)} %select_bitcast_fusion), custom_call_target="InvertDiagBlocksLowerTriangular" | custom-call | tf_op jit(solution)/shard_map/jit(_solve_triangular)/vmap()/triangular_solve | solution.py:42
  267.1 2.3 fusion.42
  269.5 38.7 %all-gather.2.cloned.1.call-done = bf16[8,64,1024]{2,1,0:T(8,128)(2,1)} async-done(((bf16[8,64,128]{2,1,0:T(8,128)(2,1)}), bf16[8,64,1024]{2,1,0:T(8,128)(2,1)}) %all-gather.2.cloned.1.call-update) | async-done | bytes 1048592 | tf_op jit(solution)/shard_map/all_gather | solution.py:43
  308.2 2.8 convolution_convert_fusion.1
  311.0 5.5 %fusion.7 = f32[36,64,64]{1,2,0:T(8,128)S(1)} fusion(bf16[36,1,64,1024]{3,2,1,0:T(8,128)(2,1)} %param.7, bf16[36,64,1024]{2,0,1:T(8,128)(2,1)S(1)} %convolution_convert_fusion.1), kind=kOutput, calls=%fused_computation.10 | convolution fusion | flops 301989888 | bytes 10027008 | tf_op jit(solution)/shard_map/eib,ekb->eik/dot_general | solution.py:51
  316.4 0.5 copy.34
  316.9 0.8 fusion.12
  317.7 1.8 fusion.17
  319.5 3.3 convolution_bitcast_fusion
  322.9 68.0 %reduce-scatter.5.cloned.1.call-done = f32[8,64,128]{2,1,0:T(8,128)} async-done(((f32[8,64,1024]{2,1,0:T(8,128)}), f32[8,64,128]{2,1,0:T(8,128)}) %reduce-scatter.5.cloned.1.call-update) | async-done | bytes 262160 | tf_op jit(solution)/shard_map/reduce_scatter | solution.py:58
  390.9 1.7 broadcast_multiply_fusion
  (16 shorter events, 0.3 us)
Async XLA Ops:
  7.2 8.2 %copy-start = (bf16[8,64,1024]{2,1,0:T(8,128)(2,1)S(1)}, bf16[8,64,1024]{2,1,0:T(8,128)(2,1)}, u32[]{:S(2)}) copy-start(bf16[8,64,1024]{2,1,0:T(8,128)(2,1)} %param.13) | copy-start | bytes 3145732
  7.2 97.3 %reduce-scatter.3.cloned.1.call-start = ((), (), s32[]{:S(2)}) async-start(), calls=%async_computation.2 | async-start | bytes 2359296 | tf_op jit(solution)/shard_map/reduce_scatter | solution.py:38
  15.4 0.7 copy-start.1
  20.3 3.8 copy-start.2
  34.2 144.3 %all-reduce.2.cloned.1.call-start = ((), (), s32[]{:S(2)}) async-start(), calls=%async_computation.3 | async-start | bytes 524288 | tf_op jit(solution)/shard_map/psum | solution.py:40
  106.9 201.3 %all-gather.2.cloned.1.call-start = ((), (), s32[]{:S(2)}) async-start(), calls=%async_computation.4 | async-start | bytes 1179648 | tf_op jit(solution)/shard_map/all_gather | solution.py:43
  269.4 121.5 %reduce-scatter.5.cloned.1.call-start = ((), (), s32[]{:S(2)}) async-start(), calls=%async_computation.5 | async-start | bytes 2359296 | tf_op jit(solution)/shard_map/reduce_scatter | solution.py:58
Sparse Core Ops, SparseCore 0:
  34.3 70.1 reduce-scatter.2
  108.4 70.0 all-reduce.1
  269.5 38.5 all-gather.1
  323.0 67.8 reduce-scatter.4
where the time goes:
time: 400 us; the launch traced here: 399 us
  waiting for transfers between devices  249 us (62%)
  other arithmetic  90.6 us (23%)
  matrix products  34.9 us (9%)
  between operations  14.6 us (4%)
  blocking collectives  7.42 us (2%)
    psum x1, waiting for transfers between devices, shards(): gram_matrix = lax.psum(gram_part, 'wide')  71.6 us
    reduce_scatter x1, waiting for transfers between devices, shards(): lax.psum_scatter(sketch, 'wide', scatter_dimension=2, tiled=True)  70.3 us
    reduce_scatter x1, waiting for transfers between devices, shards(): lax.psum_scatter(partial_rows, 'wide', scatter_dimension=2, tiled=True)  68 us
    another operation x4, other arithmetic, shards(): lower_factor = jnp.linalg.cholesky(gram_matrix)  47.1 us
    another operation x3, other arithmetic, shards(): jax.scipy.linalg.solve_triangular(lower_factor, sketch_part, lower=True)  39.4 us
    all_gather x1, waiting for transfers between devices, shards(): lax.all_gather(own_basis.astype(jnp.bfloat16), 'wide', axis=2, tiled=True)  38.7 us
    dot_general x1, matrix products, shards(): jnp.einsum('et,eib->tib', pick_target, contributions, precision=highest)  10.1 us
  transfers between devices with their start and end apart: 4, of which 4 were waited for; matrix products, arithmetic and copies ran while one was open for 0% of the time, Pallas kernels for 0%

commit v1 on v0

--- a/solution.py
+++ b/solution.py
@@ -37,7 +37,7 @@
     share_cols = full_width // wide_count
     sketch_part = lax.psum_scatter(sketch, "wide", scatter_dimension=2, tiled=True)
     gram_part = jnp.einsum("tib,tjb->tij", sketch_part, sketch_part, precision=highest)
-    gram_matrix = lax.psum(gram_part, "wide")
+    gram_matrix = jnp.sum(lax.all_gather(gram_part, "wide"), axis=0)
     lower_factor = jnp.linalg.cholesky(gram_matrix)
     own_basis = jax.scipy.linalg.solve_triangular(lower_factor, sketch_part, lower=True)
     basis_round = lax.all_gather(own_basis.astype(jnp.bfloat16), "wide", axis=2, tiled=True)

time: 400 us -> 375 us (0.938)
  waiting for transfers between devices: 249 us -> 225 us
    psum x1 -> x0, waiting for transfers between devices: 71.6 us -> none  [shards(): gram_matrix = lax.psum(gram_part, 'wide')]
    all_gather x0 -> x1, waiting for transfers between devices: none -> 48.3 us  [shards(): gram_matrix = jnp.sum(lax.all_gather(gram_part, 'wide'), axis=0)]
where the time goes in v1:
time: 375 us; the launch traced here: 374 us
  waiting for transfers between devices  225 us (60%)
  other arithmetic  91.4 us (24%)
  matrix products  34 us (9%)
  between operations  14.6 us (4%)
  blocking collectives  7.42 us (2%)
    reduce_scatter x1, waiting for transfers between devices, shards(): lax.psum_scatter(sketch, 'wide', scatter_dimension=2, tiled=True)  70.3 us
    reduce_scatter x1, waiting for transfers between devices, shards(): lax.psum_scatter(partial_rows, 'wide', scatter_dimension=2, tiled=True)  68 us
    all_gather x1, waiting for transfers between devices, shards(): gram_matrix = jnp.sum(lax.all_gather(gram_part, 'wide'), axis=0)  48.3 us
    another operation x4, other arithmetic, shards(): lower_factor = jnp.linalg.cholesky(gram_matrix)  47.1 us
    another operation x3, other arithmetic, shards(): jax.scipy.linalg.solve_triangular(lower_factor, sketch_part, lower=True)  39.4 us
    all_gather x1, waiting for transfers between devices, shards(): lax.all_gather(own_basis.astype(jnp.bfloat16), 'wide', axis=2, tiled=True)  38 us
    dot_general x1, matrix products, shards(): jnp.einsum('et,eib->tib', pick_target, contributions, precision=highest)  10.1 us
  transfers between devices with their start and end apart: 4, of which 4 were waited for; matrix products, arithmetic and copies ran while one was open for 0% of the time, Pallas kernels for 0%

profile of v1, /device:TPU:0, one launch (start us, length us, event | category | flops | bytes accessed | tf_op | source)
XLA Modules:
  0.0 374.2 jit_solution(17686704222890137244)
XLA Ops:
  7.2 0.7 fusion.36
  8.0 7.4 %all_gather.12 = bf16[2,64,1024]{2,1,0:T(8,128)(2,1)S(1)} all-gather(bf16[2,64,256]{2,1,0:T(8,128)(2,1)} %param.11), channel_id=1, replica_groups=mesh['wide'=8,'narrow'=4] {'narrow'}, dimensions={2}, use_global_device_ids=true | all-gather | bytes 327680 | tf_op jit(solution)/shard_map/all_gather | solution.py:24
  15.4 0.5 convolution_bitcast_fusion.1
  15.9 0.2 copy-done.2
  16.1 1.4 fusion.14
  17.5 0.2 copy.33
  17.7 0.3 reshape.98
  18.7 0.7 compare_select_fusion
  19.3 0.3 convolution_convert_fusion
  19.6 0.6 reshape.99
  20.3 3.8 %fusion.4 = f32[36,64,1024]{2,1,0:T(8,128)S(1)} fusion(bf16[36,64,64]{2,1,0:T(8,128)(2,1)S(1)} %reshape.99, bf16[36,1,64,1024]{3,2,1,0:T(8,128)(2,1)} %param.7), kind=kOutput, calls=%fused_computation.4 | convolution fusion | flops 301989888 | bytes 14450688 | tf_op jit(solution)/shard_map/eji,ejb->eib/dot_general | solution.py:34
  24.0 10.1 %fusion = f32[8,64,1024]{2,0,1:T(8,128)} fusion(f32[36,64,1024]{2,1,0:T(8,128)S(1)} %fusion.4, s32[36]{0:T(128)S(1)} %bitcast.80), kind=kOutput, calls=%fused_computation | convolution fusion | flops 226492704 | bytes 11534480 | tf_op jit(solution)/shard_map/et,eib->tib/dot_general | solution.py:35
  34.2 70.3 %reduce-scatter.3.cloned.1.call-done = f32[8,64,128]{2,0,1:T(8,128)} async-done(((f32[8,64,1024]{2,0,1:T(8,128)}), f32[8,64,128]{2,0,1:T(8,128)}) %reduce-scatter.3.cloned.1.call-update) | async-done | bytes 262160 | tf_op jit(solution)/shard_map/reduce_scatter | solution.py:38
  104.5 2.4 fusion.25
  106.9 0.0 all-gather.4.cloned.1.call-start
  107.0 48.3 %all-gather.6.cloned.1.call-done = f32[64,64,64]{2,1,0:T(8,128)} async-done(((f32[8,64,64]{2,1,0:T(8,128)}), f32[64,64,64]{2,1,0:T(8,128)}) %all-gather.6.cloned.1.call-update) | async-done | bytes 1048592 | tf_op jit(solution)/shard_map/all_gather | solution.py:40
  155.3 1.8 reduce_sum.9
  157.2 0.1 copy.38
  157.3 46.9 %custom-call.8 = f32[8,64,64]{2,1,0:T(8,128)S(1)} custom-call(f32[8,64,64]{2,1,0:T(8,128)S(1)} %fusion.22), custom_call_target="Cholesky" | custom-call | tf_op jit(solution)/shard_map/jit(cholesky)/cholesky | solution.py:41
  204.3 0.1 compare_reduce_fusion
  204.4 0.1 select_bitcast_fusion
  204.5 39.3 %custom-call.9 = f32[8,1,64,64]{2,3,1,0:T(8,128)S(1)} custom-call(f32[8,1,64,64]{3,2,1,0:T(8,128)S(1)} %select_bitcast_fusion), custom_call_target="InvertDiagBlocksLowerTriangular" | custom-call | tf_op jit(solution)/shard_map/jit(_solve_triangular)/vmap()/triangular_solve | solution.py:42
  243.9 1.3 fusion.42
  245.3 38.0 %all-gather.4.cloned.1.call-done = bf16[8,64,1024]{2,1,0:T(8,128)(2,1)} async-done(((bf16[8,64,128]{2,1,0:T(8,128)(2,1)}), bf16[8,64,1024]{2,1,0:T(8,128)(2,1)}) %all-gather.4.cloned.1.call-update) | async-done | bytes 1048592 | tf_op jit(solution)/shard_map/all_gather | solution.py:43
  283.3 2.8 convolution_convert_fusion.1
  286.1 5.5 %fusion.7 = f32[36,64,64]{1,2,0:T(8,128)S(1)} fusion(bf16[36,1,64,1024]{3,2,1,0:T(8,128)(2,1)} %param.7, bf16[36,64,1024]{2,0,1:T(8,128)(2,1)S(1)} %convolution_convert_fusion.1), kind=kOutput, calls=%fused_computation.10 | convolution fusion | flops 301989888 | bytes 10027008 | tf_op jit(solution)/shard_map/eib,ekb->eik/dot_general | solution.py:51
  291.6 0.5 copy.43
  292.1 0.8 fusion.12
  292.8 1.8 fusion.17
  294.7 3.3 convolution_bitcast_fusion
  298.0 68.0 %reduce-scatter.5.cloned.1.call-done = f32[8,64,128]{2,1,0:T(8,128)} async-done(((f32[8,64,1024]{2,1,0:T(8,128)}), f32[8,64,128]{2,1,0:T(8,128)}) %reduce-scatter.5.cloned.1.call-update) | async-done | bytes 262160 | tf_op jit(solution)/shard_map/reduce_scatter | solution.py:58
  366.0 1.7 broadcast_multiply_fusion
  (19 shorter events, 0.3 us)
Async XLA Ops:
  7.2 8.2 %copy-start = (bf16[8,64,1024]{2,1,0:T(8,128)(2,1)S(1)}, bf16[8,64,1024]{2,1,0:T(8,128)(2,1)}, u32[]{:S(2)}) copy-start(bf16[8,64,1024]{2,1,0:T(8,128)(2,1)} %param.13) | copy-start | bytes 3145732
  7.2 97.3 %reduce-scatter.3.cloned.1.call-start = ((), (), s32[]{:S(2)}) async-start(), calls=%async_computation.2 | async-start | bytes 2359296 | tf_op jit(solution)/shard_map/reduce_scatter | solution.py:38
  15.4 0.7 copy-start.2
  20.2 3.8 %copy-start.3 = (s32[36,1]{0,1:T(1,128)S(1)}, s32[36,1]{0,1:T(1,128)}, u32[]{:S(2)}) copy-start(s32[36,1]{0,1:T(1,128)} %param.9) | copy-start | bytes 436
  34.2 121.1 %all-gather.6.cloned.1.call-start = ((), (), s32[]{:S(2)}) async-start(), calls=%async_computation.5 | async-start | bytes 2359296 | tf_op jit(solution)/shard_map/all_gather | solution.py:40
  104.5 139.3 %copy-start.1 = (f32[8,64,128]{2,0,1:T(8,128)S(1)}, f32[8,64,128]{2,0,1:T(8,128)}, u32[]{:S(2)}) copy-start(f32[8,64,128]{2,0,1:T(8,128)} %reduce-scatter.3.cloned.1.call-done) | copy-start | bytes 786436
  106.9 176.4 %all-gather.4.cloned.1.call-start = ((), (), s32[]{:S(2)}) async-start(), calls=%async_computation.3 | async-start | bytes 1179648 | tf_op jit(solution)/shard_map/all_gather | solution.py:43
  245.2 120.8 %reduce-scatter.5.cloned.1.call-start = ((), (), s32[]{:S(2)}) async-start(), calls=%async_computation.4 | async-start | bytes 2359296 | tf_op jit(solution)/shard_map/reduce_scatter | solution.py:58
Sparse Core Ops, SparseCore 0:
  34.3 70.1 reduce-scatter.2
  107.2 48.0 all-gather.5
  245.3 37.9 all-gather.3
  298.1 67.8 reduce-scatter.4
